TPU v7x, 32 devices: a whole 2x2x4 slice. The times are simulated.
32 devices in a mesh: dp: 8 (over z, core), tensor: 4 (over y, x).
Axes of the slice: x: 2, y: 2, z: 4, core: 2. Of those that a mesh axis runs over, the one named last changes fastest.
Arguments:
- layer_input: bfloat16 [16384, 1024], P(('dp', 'tensor')), may hold values from -6 to 6
- segment_ids: int32 [32, 512], P('dp'), may hold values from 0 to 15, never falling along the last dimension, each value on 1 to 256 neighbouring positions
- w_qkv: bfloat16 [3, 1024, 1024], P(None, None, 'tensor'), may hold values from -0.1875 to 0.1875
- b_qv: bfloat16 [2, 1024], P(None, 'tensor'), may hold values from -3 to 3
- w_out: bfloat16 [1024, 1024], P('tensor'), may hold values from -0.5 to 0.5
- b_out: bfloat16 [1024], replicated, may hold values from -3 to 3
- ln1_gain: float32 [1024], replicated, may hold values from 0.5 to 1.5
- ln1_bias: float32 [1024], replicated, may hold values from -2 to 2
- w_up: bfloat16 [1024, 4096], P(None, 'tensor'), may hold values from -0.1875 to 0.1875
- b_up: bfloat16 [4096], P('tensor'), may hold values from -3 to 3
- w_down: bfloat16 [4096, 1024], P('tensor'), may hold values from -0.09375 to 0.09375
- b_down: bfloat16 [1024], replicated, may hold values from -2 to 2
- ln2_gain: float32 [1024], replicated, may hold values from 0.5 to 1.5
- ln2_bias: float32 [1024], replicated, may hold values from -2 to 2
- cotangent: bfloat16 [16384, 1024], P(('dp', 'tensor')), may hold values from -6 to 6
Outputs:
- output: bfloat16 [16384, 1024], P(('dp', 'tensor'))
- grad_input: float32 [16384, 1024], P(('dp', 'tensor'))
- grad_w_qkv: float32 [3, 1024, 1024], P(None, None, 'tensor')
- grad_b_qv: float32 [2, 1024], P(None, 'tensor')
- grad_w_out: float32 [1024, 1024], P('tensor')
- grad_b_out: float32 [1024], replicated
- grad_ln1_gain: float32 [1024], replicated
- grad_ln1_bias: float32 [1024], replicated
- grad_w_up: float32 [1024, 4096], P(None, 'tensor')
- grad_b_up: float32 [4096], P('tensor')
- grad_w_down: float32 [4096, 1024], P('tensor')
- grad_b_down: float32 [1024], replicated
- grad_ln2_gain: float32 [1024], replicated
- grad_ln2_bias: float32 [1024], replicated
Inputs may be any that keep to these rules, and one draw needn't show every extreme that they name: `segment_ids`: within a sequence the ids never fall; a document has at most 256 tokens.
All inputs are finite; a program needn't handle non-finite values.
Results may differ from a plain program's by a relative error of at most 0.018.
Values may be sent and summed in bfloat16 or wider, within the bound.
No kernel may reach another device: no remote copies, remote signals or barrier semaphores. Data moves between devices by JAX's collectives and lax.ppermute only.
A program may use at most 128 MiB of HBM per device.

v0:
```python
import jax
import jax.numpy as jnp
from jax import lax
from jax.sharding import PartitionSpec as P

HEAD_DIM = 64
norm_epsilon = 1e-05
root_half = 0.7071067811865476
inverse_root_two_pi = 0.3989422804014327


def layer_norm(token_rows, norm_gain, norm_bias):
    row_mean = jnp.mean(token_rows, -1, keepdims=True)
    centered = token_rows - row_mean
    variance = jnp.mean(centered * centered, -1, keepdims=True)
    inv_std = lax.rsqrt(variance + norm_epsilon)
    scaled = centered * inv_std
    return (scaled * norm_gain + norm_bias, scaled, inv_std)


def norm_back(incoming, scaled, inv_std, norm_gain):
    weighted = incoming * norm_gain
    d_rows = inv_std * (
        weighted
        - jnp.mean(weighted, -1, keepdims=True)
        - scaled * jnp.mean(weighted * scaled, -1, keepdims=True)
    )
    return (d_rows, jnp.sum(incoming * scaled, 0), jnp.sum(incoming, 0))


def gelu_value(up_proj):
    return 0.5 * up_proj * (1.0 + lax.erf(up_proj * root_half))


def gelu_slope(up_proj):
    return (
        0.5 * (1.0 + lax.erf(up_proj * root_half))
        + up_proj * jnp.exp(-0.5 * up_proj * up_proj) * inverse_root_two_pi
    )


def split_heads(matrix, head_count):
    return matrix.reshape(matrix.shape[0], head_count, -1)


def project(token_rows, w_qkv, b_qv):
    queries = (
        jnp.dot(token_rows, w_qkv[0], preferred_element_type=jnp.float32)
        + b_qv[0].astype(jnp.float32)
    ).astype(jnp.bfloat16)
    keys_low = jnp.dot(token_rows, w_qkv[1], preferred_element_type=jnp.float32).astype(
        jnp.bfloat16
    )
    values = (
        jnp.dot(token_rows, w_qkv[2], preferred_element_type=jnp.float32)
        + b_qv[1].astype(jnp.float32)
    ).astype(jnp.bfloat16)
    return (queries, keys_low, values)


def scores(queries, keys_low, segment, head_count, score_scale):
    raw = jnp.einsum(
        "qhd,khd->hqk",
        split_heads(queries, head_count),
        split_heads(keys_low, head_count),
        preferred_element_type=jnp.float32,
    )
    same_doc = segment[:, None] == segment[None, :]
    return jnp.where(same_doc[None], raw * score_scale, -1e30)


def mix_values(prob_low, values, head_count):
    context = jnp.einsum(
        "hqk,khd->qhd",
        prob_low,
        split_heads(values, head_count),
        preferred_element_type=jnp.float32,
    )
    return context.reshape(context.shape[0], -1).astype(jnp.bfloat16)


def ffn_forward(normed_low, up_weight, up_bias, down_weight):
    up_proj = jnp.dot(normed_low, up_weight, preferred_element_type=jnp.float32) + up_bias.astype(
        jnp.float32
    )
    activation = gelu_value(up_proj).astype(jnp.bfloat16)
    return jnp.dot(activation, down_weight, preferred_element_type=jnp.float32)


def ffn_backward(normed_low, branch_low, up_weight, up_bias, down_weight):
    up_proj = jnp.dot(normed_low, up_weight, preferred_element_type=jnp.float32) + up_bias.astype(
        jnp.float32
    )
    activation = gelu_value(up_proj).astype(jnp.bfloat16)
    grad_down = jnp.einsum("tf,td->fd", activation, branch_low, preferred_element_type=jnp.float32)
    d_activation = jnp.einsum(
        "td,fd->tf", branch_low, down_weight, preferred_element_type=jnp.float32
    )
    d_up = (d_activation * gelu_slope(up_proj)).astype(jnp.bfloat16)
    grad_up = jnp.einsum("td,tf->df", normed_low, d_up, preferred_element_type=jnp.float32)
    grad_up_bias = jnp.sum(d_up.astype(jnp.float32), 0)
    return (grad_up, grad_up_bias, grad_down, d_up)


def local(
    layer_input,
    segment_ids,
    w_qkv,
    b_qv,
    w_out,
    b_out,
    ln1_gain,
    ln1_bias,
    w_up,
    b_up,
    w_down,
    b_down,
    ln2_gain,
    ln2_bias,
    cotangent,
):
    my_rows, model_width = layer_input.shape
    seq_len = segment_ids.shape[1]
    score_scale = HEAD_DIM ** (-0.5)
    whole_input = lax.all_gather(layer_input, "tensor", axis=0, tiled=True)
    seq_input = whole_input.reshape(segment_ids.shape[0], seq_len, model_width)
    attn_width = w_out.shape[0]
    head_count = attn_width // HEAD_DIM

    def forward_seq(running, seq_item):
        token_rows, segment = seq_item
        queries, keys_low, values = project(token_rows, w_qkv, b_qv)
        logits = scores(queries, keys_low, segment, head_count, score_scale)
        row_max = jnp.max(logits, -1, keepdims=True)
        exponent = jnp.exp(logits - row_max)
        expo_sum = jnp.sum(exponent, -1, keepdims=True)
        prob_low = (exponent / expo_sum).astype(jnp.bfloat16)
        return (running, (mix_values(prob_low, values, head_count), row_max + jnp.log(expo_sum)))

    _, (seq_context, seq_lse) = lax.scan(forward_seq, None, (seq_input, segment_ids))
    all_context = seq_context.reshape(-1, attn_width)
    attention = lax.psum_scatter(
        jnp.dot(all_context, w_out, preferred_element_type=jnp.float32),
        "tensor",
        scatter_dimension=0,
        tiled=True,
    ) + b_out.astype(jnp.float32)
    normed_one, scaled_one, inv_one = layer_norm(
        layer_input.astype(jnp.float32) + attention, ln1_gain, ln1_bias
    )
    normed_low = normed_one.astype(jnp.bfloat16)
    whole_normed = lax.all_gather(normed_low, "tensor", axis=0, tiled=True)
    branch = lax.psum_scatter(
        ffn_forward(whole_normed, w_up, b_up, w_down), "tensor", scatter_dimension=0, tiled=True
    )
    normed_two, scaled_two, inv_two = layer_norm(
        normed_one + branch + b_down.astype(jnp.float32), ln2_gain, ln2_bias
    )
    d_second, grad_ln2_gain, grad_ln2_bias = norm_back(
        cotangent.astype(jnp.float32), scaled_two, inv_two, ln2_gain
    )
    branch_low = d_second.astype(jnp.bfloat16)
    grad_b_down = jnp.sum(branch_low.astype(jnp.float32), 0)
    whole_branch = lax.all_gather(branch_low, "tensor", axis=0, tiled=True)
    grad_w_up, grad_b_up, grad_w_down, d_up = ffn_backward(
        whole_normed, whole_branch, w_up, b_up, w_down
    )
    d_normed = lax.psum_scatter(
        jnp.einsum("tf,df->td", d_up, w_up, preferred_element_type=jnp.float32),
        "tensor",
        scatter_dimension=0,
        tiled=True,
    )
    d_first, grad_ln1_gain, grad_ln1_bias = norm_back(
        d_second + d_normed, scaled_one, inv_one, ln1_gain
    )
    attention_low = d_first.astype(jnp.bfloat16)
    grad_b_out = jnp.sum(attention_low.astype(jnp.float32), 0)
    whole_grad = lax.all_gather(attention_low, "tensor", axis=0, tiled=True)
    seq_grad = whole_grad.reshape(seq_input.shape[0], seq_len, model_width)

    def backward_seq(running, seq_item):
        grad_qkv, grad_bias, grad_out = running
        token_rows, segment, seq_lse_one, grad_rows = seq_item
        queries, keys_low, values = project(token_rows, w_qkv, b_qv)
        logits = scores(queries, keys_low, segment, head_count, score_scale)
        probability = jnp.exp(logits - seq_lse_one)
        prob_low = probability.astype(jnp.bfloat16)
        context = mix_values(prob_low, values, head_count)
        grad_out = grad_out + jnp.einsum(
            "te,td->ed", context, grad_rows, preferred_element_type=jnp.float32
        )
        d_context = jnp.einsum(
            "td,ed->te", grad_rows, w_out, preferred_element_type=jnp.float32
        ).astype(jnp.bfloat16)
        d_heads = split_heads(d_context, head_count)
        d_prob = jnp.einsum(
            "qhd,khd->hqk",
            d_heads,
            split_heads(values, head_count),
            preferred_element_type=jnp.float32,
        )
        d_values = (
            jnp.einsum("hqk,qhd->khd", prob_low, d_heads, preferred_element_type=jnp.float32)
            .reshape(seq_len, -1)
            .astype(jnp.bfloat16)
        )
        inner_sum = jnp.sum(probability * d_prob, -1, keepdims=True)
        d_raw = (probability * (d_prob - inner_sum) * score_scale).astype(jnp.bfloat16)
        d_queries = (
            jnp.einsum(
                "hqk,khd->qhd",
                d_raw,
                split_heads(keys_low, head_count),
                preferred_element_type=jnp.float32,
            )
            .reshape(seq_len, -1)
            .astype(jnp.bfloat16)
        )
        d_keys = (
            jnp.einsum(
                "hqk,qhd->khd",
                d_raw,
                split_heads(queries, head_count),
                preferred_element_type=jnp.float32,
            )
            .reshape(seq_len, -1)
            .astype(jnp.bfloat16)
        )
        grad_qkv = grad_qkv + jnp.stack(
            [
                jnp.einsum("td,te->de", token_rows, gradient, preferred_element_type=jnp.float32)
                for gradient in (d_queries, d_keys, d_values)
            ]
        )
        grad_bias = grad_bias + jnp.stack(
            [jnp.sum(d_queries.astype(jnp.float32), 0), jnp.sum(d_values.astype(jnp.float32), 0)]
        )
        return ((grad_qkv, grad_bias, grad_out), (d_queries, d_keys, d_values))

    start_grads = (
        jnp.zeros((3, model_width, attn_width), jnp.float32),
        jnp.zeros((2, attn_width), jnp.float32),
        jnp.zeros((attn_width, model_width), jnp.float32),
    )
    (grad_w_qkv, grad_b_qv, grad_w_out), seq_d = lax.scan(
        backward_seq, start_grads, (seq_input, segment_ids, seq_lse, seq_grad)
    )
    all_d = [gradient.reshape(-1, attn_width) for gradient in seq_d]
    summed = jnp.zeros((my_rows * lax.axis_size("tensor"), model_width), jnp.float32)
    for which in range(3):
        piece = all_d[which]
        summed = summed + jnp.einsum(
            "te,de->td", piece, w_qkv[which], preferred_element_type=jnp.float32
        )
    grad_input = d_first + lax.psum_scatter(
        summed.astype(jnp.bfloat16), "tensor", scatter_dimension=0, tiled=True
    ).astype(jnp.float32)
    grad_w_qkv, grad_b_qv, grad_w_out, grad_w_up, grad_b_up, grad_w_down = (
        lax.psum(grad_w_qkv.astype(jnp.bfloat16), "dp").astype(jnp.float32),
        lax.psum(grad_b_qv.astype(jnp.bfloat16), "dp").astype(jnp.float32),
        lax.psum(grad_w_out.astype(jnp.bfloat16), "dp").astype(jnp.float32),
        lax.psum(grad_w_up.astype(jnp.bfloat16), "dp").astype(jnp.float32),
        lax.psum(grad_b_up.astype(jnp.bfloat16), "dp").astype(jnp.float32),
        lax.psum(grad_w_down.astype(jnp.bfloat16), "dp").astype(jnp.float32),
    )
    grad_b_out, grad_ln1_gain, grad_ln1_bias, grad_b_down, grad_ln2_gain, grad_ln2_bias = lax.psum(
        (grad_b_out, grad_ln1_gain, grad_ln1_bias, grad_b_down, grad_ln2_gain, grad_ln2_bias),
        ("dp", "tensor"),
    )
    return (
        normed_two.astype(jnp.bfloat16),
        grad_input,
        grad_w_qkv,
        grad_b_qv,
        grad_w_out,
        grad_b_out,
        grad_ln1_gain,
        grad_ln1_bias,
        grad_w_up,
        grad_b_up,
        grad_w_down,
        grad_b_down,
        grad_ln2_gain,
        grad_ln2_bias,
    )


def solution(mesh):
    return jax.shard_map(
        local,
        mesh=mesh,
        in_specs=(
            P(("dp", "tensor"), None),
            P("dp", None),
            P(None, None, "tensor"),
            P(None, "tensor"),
            P("tensor", None),
            P(),
            P(),
            P(),
            P(None, "tensor"),
            P("tensor"),
            P("tensor", None),
            P(),
            P(),
            P(),
            P(("dp", "tensor"), None),
        ),
        out_specs=(
            P(("dp", "tensor"), None),
            P(("dp", "tensor"), None),
            P(None, None, "tensor"),
            P(None, "tensor"),
            P("tensor", None),
            P(),
            P(),
            P(),
            P(None, "tensor"),
            P("tensor"),
            P("tensor", None),
            P(),
            P(),
            P(),
        ),
        check_vma=False,
    )
```

profile of v0, /device:TPU:0, one launch (start us, length us, event | category | flops | bytes accessed | tf_op | source)
XLA Modules:
  0.0 977.5 jit_solution(15801574085958323130)
XLA Ops:
  8.0 57.3 %all-gather.5.cloned.1.call-done = bf16[2048,1024]{1,0:T(8,128)(2,1)} async-done(((bf16[512,1024]{1,0:T(8,128)(2,1)}), bf16[2048,1024]{1,0:T(8,128)(2,1)}) %all-gather.5.cloned.1.call-update) | async-done | bytes 4194320 | tf_op jit(solution)/shard_map/all_gather | solution.py:125
  66.4 45.4 %while.33 = (s32[]{:T(128)}, bf16[4,512,256]{2,1,0:T(8,128)(2,1)}, f32[4,4,512,1]{2,1,3,0:T(4,128)S(1)}, bf16[4,512,1024]{2,1,0:T(8,128)(2,1)}, bf16[3,1024,256]...) while((s32[]{:T(128)}, bf16[4,512,256]{2,1,0:T(8,128)(2,1)}, ...), condition=%wide.region_3.4_spmd, body=%wide.region_0.3_spmd.sunk | while | flops 1087371776 | bytes 21310580 | solution.py:140
  111.8 5.8 fusion.111
  118.3 85.9 %reduce-scatter.5.cloned.1.call-done = f32[512,1024]{1,0:T(8,128)} async-done(((f32[2048,1024]{1,0:T(8,128)}), f32[512,1024]{1,0:T(8,128)}) %reduce-scatter.5.cloned.1.call-update) | async-done | bytes 2097168 | tf_op jit(solution)/shard_map/reduce_scatter | solution.py:142
  208.9 52.8 %all-gather.7.cloned.1.call-done = bf16[2048,1024]{1,0:T(8,128)(2,1)} async-done(((bf16[512,1024]{1,0:T(8,128)(2,1)}), bf16[2048,1024]{1,0:T(8,128)(2,1)}) %all-gather.7.cloned.1.call-update) | async-done | bytes 4194320 | tf_op jit(solution)/shard_map/all_gather | solution.py:152
  261.7 8.9 multiply_convert_fusion.1
  272.7 6.6 fusion.112
  280.0 85.9 %reduce-scatter.7.cloned.1.call-done = f32[512,1024]{1,0:T(8,128)} async-done(((f32[2048,1024]{1,0:T(8,128)}), f32[512,1024]{1,0:T(8,128)}) %reduce-scatter.7.cloned.1.call-update) | async-done | bytes 2097168 | tf_op jit(solution)/shard_map/reduce_scatter | solution.py:153
  373.1 52.8 %all-gather.9.cloned.1.call-done = bf16[2048,1024]{1,0:T(8,128)(2,1)} async-done(((bf16[512,1024]{1,0:T(8,128)(2,1)}), bf16[2048,1024]{1,0:T(8,128)(2,1)}) %all-gather.9.cloned.1.call-update) | async-done | bytes 4194320 | tf_op jit(solution)/shard_map/all_gather | solution.py:164
  425.9 11.3 %fusion.109 = (bf16[1024]{0:T(1024)(128)(2,1)S(1)}, bf16[2048,1024]{1,0:T(8,128)(2,1)S(1)}) fusion(f32[2048,1024]{1,0:T(8,128)} %get-tuple-element.268, f32[1024]{0:T(1024)S(1)} %convert_element_type.218, bf16[2048,1024]{1,0:T(8,128)(2,1)} %all-gather.9.cloned.1.call-done, bf16[1024,1024]{1,0:T(8,128)(2,1)} %param.29), kind=kOutput, calls=%fused_computation.164 | convolution fusion | flops 4320132096 | bytes 18880512 | tf_op jit(solution)/shard_map/td,fd->tf/dot_general | solution.py:96
  439.2 7.0 fusion.113
  446.3 86.5 %reduce-scatter.9.cloned.1.call-done = f32[512,1024]{1,0:T(8,128)} async-done(((f32[2048,1024]{1,0:T(8,128)}), f32[512,1024]{1,0:T(8,128)}) %reduce-scatter.9.cloned.1.call-update) | async-done | bytes 2097168 | tf_op jit(solution)/shard_map/reduce_scatter | solution.py:168
  532.8 4.5 multiply_reduce_fusion.1
  539.8 9.5 convolution_convert_fusion.5
  549.3 6.0 convolution_convert_fusion.6
  555.3 37.3 %all-gather.11.cloned.1.call-done = bf16[2048,1024]{1,0:T(8,128)(2,1)} async-done(((bf16[512,1024]{1,0:T(8,128)(2,1)}), bf16[2048,1024]{1,0:T(8,128)(2,1)}) %all-gather.11.cloned.1.call-update) | async-done | bytes 4194320 | tf_op jit(solution)/shard_map/all_gather | solution.py:179
  595.7 172.4 %while.34 = (s32[]{:T(128)}, f32[3,1024,256]{2,1,0:T(8,128)}, f32[2,256]{1,0:T(2,128)S(1)}, f32[256,1024]{1,0:T(8,128)S(1)}, bf16[4,512,256]{2,1,0:T(8,128)(2,1)...) while((s32[]{:T(128)}, f32[3,1024,256]{2,1,0:T(8,128)}, ...), condition=%wide.region_19.20_spmd.clone, body=%wide.region_15.19_spmd.clone.sunk | while | flops 2974292480 | bytes 91798968 | solution.py:246
  614.7 7.1 fusion.236
  621.8 7.3 convert_reduce_fusion.8
  656.4 7.1 fusion.236
  663.5 7.3 convert_reduce_fusion.8
  676.1 4.0 maximum_add_fusion.4
  700.0 7.1 fusion.236
  707.1 7.3 convert_reduce_fusion.8
  719.7 4.0 maximum_add_fusion.4
  743.6 7.1 fusion.236
  750.7 7.3 convert_reduce_fusion.8
  763.2 4.0 maximum_add_fusion.4
  781.3 41.4 %all-reduce = (f32[1024]{0:T(1024)}, f32[1024]{0:T(1024)}, f32[1024]{0:T(1024)}, f32[1024]{0:T(1024)}, f32[1024]{0:T(1024)}, /*index=5*/f32[1024]{0:T(1024)}) all-reduce(f32[1024]{0:T(1024)S(1)} %get-tuple-element.246, f32[1024]{0:T(1024)S(1)} %get-tuple-element.182, ...), channel_id=1, replica_groups=mesh['dp'=8,'tensor'=4] {'dp','tensor'}, use_global_device_ids=true, to_apply=%region_25.26 | all-reduce | flops 6144 | bytes 49152 | tf_op jit(solution)/shard_map/psum | solution.py:267
  822.7 16.7 %all-reduce.1 = (bf16[2,256]{1,0:T(2,128)(2,1)S(1)}, bf16[1024]{0:T(1024)(128)(2,1)S(1)}) all-reduce(bf16[2,256]{1,0:T(2,128)(2,1)S(1)} %convert_element_type.230, bf16[1024]{0:T(1024)(128)(2,1)S(1)} %get-tuple-element.269), channel_id=1, replica_groups=mesh['dp'=8,'tensor'=4] {'dp'}, use_global_device_ids=true, to_apply=%region_22.23 | all-reduce | flops 1536 | bytes 6144 | tf_op jit(solution)/shard_map/psum | solution.py:261
  840.5 70.3 %all-reduce.5.cloned.1.call-done = (bf16[3,1024,256]{2,1,0:T(8,128)(2,1)}, bf16[256,1024]{1,0:T(8,128)(2,1)}, bf16[1024,1024]{1,0:T(8,128)(2,1)}, bf16[1024,1024]{1,0:T(8,128)(2,1)}) async-done(((bf16[3,1024,256]{2,1,0:T(8,128)(2,1)}, bf16[256,1024]{1,0:T(8,128)(2,1)}, bf16[1024,1024]{1,0:T(8,128)(2,1)}, bf16[1024,1024]{1,0:T(8,128)(2,1)}), (bf16[3,1024,256]{2,1,0:T(8,128)(2,1)}, ...) | async-done | bytes 6291472 | tf_op jit(solution)/shard_map/psum | solution.py:260
  921.6 45.3 %reduce-scatter.11.cloned.1.call-done = bf16[512,1024]{1,0:T(8,128)(2,1)} async-done(((bf16[2048,1024]{1,0:T(8,128)(2,1)}), bf16[512,1024]{1,0:T(8,128)(2,1)}) %reduce-scatter.11.cloned.1.call-update) | async-done | bytes 1048592 | tf_op jit(solution)/shard_map/reduce_scatter | solution.py:256
  (324 shorter events, 200.8 us)
Async XLA Ops:
  7.2 254.5 %copy-start = (bf16[1024,1024]{1,0:T(8,128)(2,1)S(1)}, bf16[1024,1024]{1,0:T(8,128)(2,1)}, u32[]{:S(2)}) copy-start(bf16[1024,1024]{1,0:T(8,128)(2,1)} %param.27) | copy-start | bytes 6291460
  7.2 58.1 %all-gather.5.cloned.1.call-start = ((), (), s32[]{:S(2)}) async-start(), calls=%async_computation.4 | async-start | bytes 5242880 | tf_op jit(solution)/shard_map/all_gather | solution.py:125
  7.9 196.3 %reduce-scatter.5.cloned.1.call-start = ((), (), s32[]{:S(2)}) async-start(), calls=%async_computation.5 | async-start | bytes 10485760 | tf_op jit(solution)/shard_map/reduce_scatter | solution.py:142
  117.6 86.6 %copy-start.13 = (bf16[512,1024]{1,0:T(8,128)(2,1)S(1)}, bf16[512,1024]{1,0:T(8,128)(2,1)}, u32[]{:S(2)}) copy-start(bf16[512,1024]{1,0:T(8,128)(2,1)} %param.19) | copy-start | bytes 3145732
  117.6 144.1 %all-gather.7.cloned.1.call-start = ((), (), s32[]{:S(2)}) async-start(), calls=%async_computation.6 | async-start | bytes 5242880 | tf_op jit(solution)/shard_map/all_gather | solution.py:152
  118.3 89.2 %copy-start.18 = (f32[1024]{0:T(1024)S(1)}, f32[1024]{0:T(1024)}, u32[]{:S(2)}) copy-start(f32[1024]{0:T(1024)} %param.25) | copy-start | bytes 12292
  118.3 89.2 %copy-start.22 = (f32[1024]{0:T(1024)S(1)}, f32[1024]{0:T(1024)}, u32[]{:S(2)}) copy-start(f32[1024]{0:T(1024)} %param.26) | copy-start | bytes 12292
  208.9 157.0 %reduce-scatter.7.cloned.1.call-start = ((), (), s32[]{:S(2)}) async-start(), calls=%async_computation.7 | async-start | bytes 10485760 | tf_op jit(solution)/shard_map/reduce_scatter | solution.py:153
  261.7 11.0 %copy-start.29 = (bf16[1024,1024]{1,0:T(8,128)(2,1)S(1)}, bf16[1024,1024]{1,0:T(8,128)(2,1)}, u32[]{:S(2)}) copy-start(bf16[1024,1024]{1,0:T(8,128)(2,1)} %param.29) | copy-start | bytes 6291460
  279.3 146.6 %all-gather.9.cloned.1.call-start = ((), (), s32[]{:S(2)}) async-start(), calls=%async_computation.8 | async-start | bytes 5242880 | tf_op jit(solution)/shard_map/all_gather | solution.py:164
  280.0 89.2 %copy-start.9 = (bf16[512,1024]{1,0:T(8,128)(2,1)S(1)}, bf16[512,1024]{1,0:T(8,128)(2,1)}, u32[]{:S(2)}) copy-start(bf16[512,1024]{1,0:T(8,128)(2,1)} %param.33) | copy-start | bytes 3145732
  280.0 89.3 %copy-start.19 = (f32[1024]{0:T(1024)S(1)}, f32[1024]{0:T(1024)}, u32[]{:S(2)}) copy-start(f32[1024]{0:T(1024)} %param.31) | copy-start | bytes 12292
  373.1 159.7 %reduce-scatter.9.cloned.1.call-start = ((), (), s32[]{:S(2)}) async-start(), calls=%async_computation.9 | async-start | bytes 10485760 | tf_op jit(solution)/shard_map/reduce_scatter | solution.py:168
  446.2 86.6 %copy-start.4 = (f32[512,1024]{1,0:T(8,128)S(1)}, f32[512,1024]{1,0:T(8,128)}, u32[]{:S(2)}) copy-start(f32[512,1024]{1,0:T(8,128)} %copy-done.3) | copy-start | bytes 6291460
  446.2 86.6 %copy-start.24 = (f32[1024]{0:T(1024)S(1)}, f32[1024]{0:T(1024)}, u32[]{:S(2)}) copy-start(f32[1024]{0:T(1024)} %param.32) | copy-start | bytes 12292
  446.3 146.3 %all-gather.11.cloned.1.call-start = ((), (), s32[]{:S(2)}) async-start(), calls=%async_computation.10 | async-start | bytes 5242880 | tf_op jit(solution)/shard_map/all_gather | solution.py:179
  539.7 371.2 %all-reduce.5.cloned.1.call-start = ((), (), s32[]{:S(2)}) async-start(), calls=%async_computation.12 | async-start | bytes 12582912 | tf_op jit(solution)/shard_map/psum | solution.py:260
  539.8 9.5 copy-start.28
  539.8 9.5 copy-start.36
  555.3 40.4 %copy-start.17 = (bf16[2,256]{1,0:T(2,128)(2,1)S(1)}, bf16[2,256]{1,0:T(2,128)(2,1)}, u32[]{:S(2)}) copy-start(bf16[2,256]{1,0:T(2,128)(2,1)} %get-tuple-element.548) | copy-start | bytes 3076
  600.4 5.1 copy-start.32
  610.2 4.5 copy-start.33
  614.7 7.1 copy-start.31
  642.0 5.1 copy-start.32
  656.4 7.1 copy-start.31
  685.6 5.1 copy-start.32
  700.0 7.1 copy-start.31
  729.2 5.1 copy-start.32
  743.6 7.1 copy-start.31
  772.2 194.7 %reduce-scatter.11.cloned.1.call-start = ((), (), s32[]{:S(2)}) async-start(), calls=%async_computation.11 | async-start | bytes 5242880 | tf_op jit(solution)/shard_map/reduce_scatter | solution.py:256
  910.9 5.6 copy-start.15
  919.0 51.6 %copy-start.1 = (bf16[1024,1024]{1,0:T(8,128)(2,1)S(1)}, bf16[1024,1024]{1,0:T(8,128)(2,1)}, u32[]{:S(2)}) copy-start(bf16[1024,1024]{1,0:T(8,128)(2,1)} %param.27) | copy-start | bytes 6291460
  (38 other events, 87.6 us)
Sparse Core Ops, SparseCore 0:
  9.9 55.3 all-gather.4
  117.7 86.4 reduce-scatter.4
  209.0 52.6 all-gather.6
  279.4 86.4 reduce-scatter.6
  373.2 52.6 all-gather.8
  446.4 86.4 reduce-scatter.8
  539.8 52.6 all-gather.10
  772.3 138.4 all-reduce.4
  914.1 52.7 reduce-scatter.10
where the time goes:
time: 988 us; the launch traced here: 978 us
  waiting for transfers between devices  575 us (58%)
  matrix products  230 us (23%)
  other arithmetic  59.9 us (6%)
  blocking collectives  58.1 us (6%)
  local copies, waits for them, and re-layouts  38 us (4%)
  between operations  14.5 us (1%)
    reduce_scatter x1, waiting for transfers between devices, local(): lax.psum_scatter(jnp.einsum('tf,df->td', d_up, w_up, preferred_element_ty...  86.5 us
    reduce_scatter x1, waiting for transfers between devices, local(): lax.psum_scatter(jnp.dot(all_context, w_out, preferred_element_type=jnp.f...  85.9 us
    reduce_scatter x1, waiting for transfers between devices, local(): lax.psum_scatter(ffn_forward(whole_normed, w_up, b_up, w_down), 'tensor',...  85.9 us
    psum x1, waiting for transfers between devices, local(): lax.psum(grad_w_qkv.astype(jnp.bfloat16), 'dp').astype(jnp.float32)  70.3 us
    all_gather x1, waiting for transfers between devices, local(): whole_input = lax.all_gather(layer_input, 'tensor', axis=0, tiled=True)  57.3 us
    all_gather x1, waiting for transfers between devices, local(): whole_branch = lax.all_gather(branch_low, 'tensor', axis=0, tiled=True)  52.8 us
    all_gather x1, waiting for transfers between devices, local(): whole_normed = lax.all_gather(normed_low, 'tensor', axis=0, tiled=True)  52.8 us
    reduce_scatter x1, waiting for transfers between devices, local(): lax.psum_scatter(summed.astype(jnp.bfloat16), 'tensor', scatter_dimension...  45.3 us
  transfers between devices with their start and end apart: 9, of which 9 were waited for; matrix products, arithmetic and copies ran while one was open for 4% of the time, Pallas kernels for 0%

commit v1 on v0

--- a/solution.py
+++ b/solution.py
@@ -2,11 +2,16 @@
 import jax.numpy as jnp
 from jax import lax
 from jax.sharding import PartitionSpec as P
+from jax.lax import all_gather
 
 HEAD_DIM = 64
 norm_epsilon = 1e-05
 root_half = 0.7071067811865476
 inverse_root_two_pi = 0.3989422804014327
+
+
+def set_balance(frame, axis_key):
+    return all_gather(frame, axis_key).sum(axis=0)
 
 
 def layer_norm(token_rows, norm_gain, norm_bias):
@@ -257,7 +262,7 @@
         summed.astype(jnp.bfloat16), "tensor", scatter_dimension=0, tiled=True
     ).astype(jnp.float32)
     grad_w_qkv, grad_b_qv, grad_w_out, grad_w_up, grad_b_up, grad_w_down = (
-        lax.psum(grad_w_qkv.astype(jnp.bfloat16), "dp").astype(jnp.float32),
+        set_balance(grad_w_qkv.astype(jnp.bfloat16), "dp").astype(jnp.float32),
         lax.psum(grad_b_qv.astype(jnp.bfloat16), "dp").astype(jnp.float32),
         lax.psum(grad_w_out.astype(jnp.bfloat16), "dp").astype(jnp.float32),
         lax.psum(grad_w_up.astype(jnp.bfloat16), "dp").astype(jnp.float32),

time: 988 us -> 1080 us (1.093)
  waiting for transfers between devices: 575 us -> 661 us
    all_gather x0 -> x1, waiting for transfers between devices: none -> 115 us  [set_balance(): return all_gather(frame, axis_key).sum(axis=0)]
    psum x1, waiting for transfers between devices: 70.3 us -> 38.9 us  [local(): lax.psum(grad_w_out.astype(jnp.bfloat16), 'dp').astype(jnp.float32)]
  transfers between devices with their start and end apart: 9 -> 10, of which waited for: 9 -> 10; matrix products, arithmetic and copies ran while one was open for 4% -> 4% of each run, Pallas kernels for 0% -> 0%
where the time goes in v1:
time: 1080 us; the launch traced here: 1070 us
  waiting for transfers between devices  661 us (61%)
  matrix products  230 us (21%)
  other arithmetic  68.7 us (6%)
  blocking collectives  57.3 us (5%)
  local copies, waits for them, and re-layouts  36.6 us (3%)
  between operations  14.9 us (1%)
    all_gather x1, waiting for transfers between devices, set_balance(): return all_gather(frame, axis_key).sum(axis=0)  115 us
    reduce_scatter x1, waiting for transfers between devices, local(): lax.psum_scatter(jnp.einsum('tf,df->td', d_up, w_up, preferred_element_ty...  86.5 us
    reduce_scatter x1, waiting for transfers between devices, local(): lax.psum_scatter(jnp.dot(all_context, w_out, preferred_element_type=jnp.f...  85.9 us
    reduce_scatter x1, waiting for transfers between devices, local(): lax.psum_scatter(ffn_forward(whole_normed, w_up, b_up, w_down), 'tensor',...  85.9 us
    all_gather x1, waiting for transfers between devices, local(): whole_input = lax.all_gather(layer_input, 'tensor', axis=0, tiled=True)  57.3 us
    all_gather x1, waiting for transfers between devices, local(): whole_branch = lax.all_gather(branch_low, 'tensor', axis=0, tiled=True)  52.8 us
    all_gather x1, waiting for transfers between devices, local(): whole_normed = lax.all_gather(normed_low, 'tensor', axis=0, tiled=True)  52.8 us
    reduce_scatter x1, waiting for transfers between devices, local(): lax.psum_scatter(summed.astype(jnp.bfloat16), 'tensor', scatter_dimension...  47.2 us
  transfers between devices with their start and end apart: 10, of which 10 were waited for; matrix products, arithmetic and copies ran while one was open for 4% of the time, Pallas kernels for 0%

profile of v1, /device:TPU:0, one launch (start us, length us, event | category | flops | bytes accessed | tf_op | source)
XLA Modules:
  0.0 1070.4 jit_solution(2534823326463418211)
XLA Ops:
  8.0 57.3 %all-gather.7.cloned.1.call-done = bf16[2048,1024]{1,0:T(8,128)(2,1)} async-done(((bf16[512,1024]{1,0:T(8,128)(2,1)}), bf16[2048,1024]{1,0:T(8,128)(2,1)}) %all-gather.7.cloned.1.call-update) | async-done | bytes 4194320 | tf_op jit(solution)/shard_map/all_gather | solution.py:130
  66.4 45.4 %while.33 = (s32[]{:T(128)}, bf16[4,512,256]{2,1,0:T(8,128)(2,1)}, f32[4,4,512,1]{2,1,3,0:T(4,128)S(1)}, bf16[4,512,1024]{2,1,0:T(8,128)(2,1)}, bf16[3,1024,256]...) while((s32[]{:T(128)}, bf16[4,512,256]{2,1,0:T(8,128)(2,1)}, ...), condition=%wide.region_3.4_spmd, body=%wide.region_0.3_spmd.sunk | while | flops 1087371776 | bytes 21310580 | solution.py:145
  111.8 5.8 fusion.111
  118.3 85.9 %reduce-scatter.5.cloned.1.call-done = f32[512,1024]{1,0:T(8,128)} async-done(((f32[2048,1024]{1,0:T(8,128)}), f32[512,1024]{1,0:T(8,128)}) %reduce-scatter.5.cloned.1.call-update) | async-done | bytes 2097168 | tf_op jit(solution)/shard_map/reduce_scatter | solution.py:147
  208.9 52.8 %all-gather.9.cloned.1.call-done = bf16[2048,1024]{1,0:T(8,128)(2,1)} async-done(((bf16[512,1024]{1,0:T(8,128)(2,1)}), bf16[2048,1024]{1,0:T(8,128)(2,1)}) %all-gather.9.cloned.1.call-update) | async-done | bytes 4194320 | tf_op jit(solution)/shard_map/all_gather | solution.py:157
  261.7 8.9 multiply_convert_fusion.1
  272.7 6.6 fusion.112
  280.0 85.9 %reduce-scatter.7.cloned.1.call-done = f32[512,1024]{1,0:T(8,128)} async-done(((f32[2048,1024]{1,0:T(8,128)}), f32[512,1024]{1,0:T(8,128)}) %reduce-scatter.7.cloned.1.call-update) | async-done | bytes 2097168 | tf_op jit(solution)/shard_map/reduce_scatter | solution.py:158
  373.1 52.8 %all-gather.11.cloned.1.call-done = bf16[2048,1024]{1,0:T(8,128)(2,1)} async-done(((bf16[512,1024]{1,0:T(8,128)(2,1)}), bf16[2048,1024]{1,0:T(8,128)(2,1)}) %all-gather.11.cloned.1.call-update) | async-done | bytes 4194320 | tf_op jit(solution)/shard_map/all_gather | solution.py:169
  425.9 11.3 %fusion.109 = (bf16[1024]{0:T(1024)(128)(2,1)S(1)}, bf16[2048,1024]{1,0:T(8,128)(2,1)S(1)}) fusion(f32[2048,1024]{1,0:T(8,128)} %get-tuple-element.267, f32[1024]{0:T(1024)S(1)} %convert_element_type.220, bf16[2048,1024]{1,0:T(8,128)(2,1)} %all-gather.11.cloned.1.call-done, bf16[1024,1024]{1,0:T(8,128)(2,1)} %param.29), kind=kOutput, calls=%fused_computation.164 | convolution fusion | flops 4320132096 | bytes 18880512 | tf_op jit(solution)/shard_map/td,fd->tf/dot_general | solution.py:101
  439.2 7.0 fusion.113
  446.3 86.5 %reduce-scatter.9.cloned.1.call-done = f32[512,1024]{1,0:T(8,128)} async-done(((f32[2048,1024]{1,0:T(8,128)}), f32[512,1024]{1,0:T(8,128)}) %reduce-scatter.9.cloned.1.call-update) | async-done | bytes 2097168 | tf_op jit(solution)/shard_map/reduce_scatter | solution.py:173
  532.8 4.5 multiply_reduce_fusion.1
  539.8 9.6 convolution_convert_fusion.5
  549.3 6.0 convolution_convert_fusion.6
  555.4 37.2 %all-gather.13.cloned.1.call-done = bf16[2048,1024]{1,0:T(8,128)(2,1)} async-done(((bf16[512,1024]{1,0:T(8,128)(2,1)}), bf16[2048,1024]{1,0:T(8,128)(2,1)}) %all-gather.13.cloned.1.call-update) | async-done | bytes 4194320 | tf_op jit(solution)/shard_map/all_gather | solution.py:184
  595.7 172.4 %while.34 = (s32[]{:T(128)}, f32[3,1024,256]{2,1,0:T(8,128)}, f32[2,256]{1,0:T(2,128)S(1)}, f32[256,1024]{1,0:T(8,128)S(1)}, bf16[4,512,256]{2,1,0:T(8,128)(2,1)...) while((s32[]{:T(128)}, f32[3,1024,256]{2,1,0:T(8,128)}, ...), condition=%wide.region_19.20_spmd.clone, body=%wide.region_15.19_spmd.clone.sunk | while | flops 2974292480 | bytes 91798968 | solution.py:251
  614.7 7.1 fusion.236
  621.8 7.3 convert_reduce_fusion.8
  656.4 7.1 fusion.236
  663.5 7.3 convert_reduce_fusion.8
  700.0 7.1 fusion.236
  707.1 7.3 convert_reduce_fusion.8
  743.5 7.1 fusion.236
  750.7 7.3 convert_reduce_fusion.8
  780.1 41.5 %all-reduce = (f32[1024]{0:T(1024)}, f32[1024]{0:T(1024)}, f32[1024]{0:T(1024)}, f32[1024]{0:T(1024)}, f32[1024]{0:T(1024)}, /*index=5*/f32[1024]{0:T(1024)}) all-reduce(f32[1024]{0:T(1024)S(1)} %get-tuple-element.245, f32[1024]{0:T(1024)S(1)} %get-tuple-element.182, ...), channel_id=1, replica_groups=mesh['dp'=8,'tensor'=4] {'dp','tensor'}, use_global_device_ids=true, to_apply=%region_25.26 | all-reduce | flops 6144 | bytes 49152 | tf_op jit(solution)/shard_map/psum | solution.py:272
  821.5 15.9 %all-reduce.1 = (bf16[2,256]{1,0:T(2,128)(2,1)S(1)}, bf16[1024]{0:T(1024)(128)(2,1)S(1)}) all-reduce(bf16[2,256]{1,0:T(2,128)(2,1)S(1)} %convert_element_type.232, bf16[1024]{0:T(1024)(128)(2,1)S(1)} %get-tuple-element.268), channel_id=1, replica_groups=mesh['dp'=8,'tensor'=4] {'dp'}, use_global_device_ids=true, to_apply=%region_22.23 | all-reduce | flops 1536 | bytes 6144 | tf_op jit(solution)/shard_map/psum | solution.py:266
  838.6 38.9 %all-reduce.5.cloned.1.call-done = (bf16[256,1024]{1,0:T(8,128)(2,1)}, bf16[1024,1024]{1,0:T(8,128)(2,1)}, bf16[1024,1024]{1,0:T(8,128)(2,1)}) async-done(((bf16[256,1024]{1,0:T(8,128)(2,1)}, bf16[1024,1024]{1,0:T(8,128)(2,1)}, bf16[1024,1024]{1,0:T(8,128)(2,1)}), (bf16[256,1024]{1,0:T(8,128)(2,1)}, bf16[1024,1024]{1,0:T(8,128)(2,1)}, bf16[1024,1024]{1,0:T(8,128)(2,1)})) %all-reduce.5.cloned.1.call-update) | async-done | bytes 4718608 | tf_op jit(solution)/shard_map/psum | solution.py:267
  879.5 4.2 convert_element_type.238
  886.2 47.2 %reduce-scatter.11.cloned.1.call-done = bf16[512,1024]{1,0:T(8,128)(2,1)} async-done(((bf16[2048,1024]{1,0:T(8,128)(2,1)}), bf16[512,1024]{1,0:T(8,128)(2,1)}) %reduce-scatter.11.cloned.1.call-update) | async-done | bytes 1048592 | tf_op jit(solution)/shard_map/reduce_scatter | solution.py:261
  936.4 115.3 %all-gather.15.cloned.1.call-done = bf16[24,1024,256]{2,1,0:T(8,128)(2,1)} async-done(((bf16[3,1024,256]{2,1,0:T(8,128)(2,1)}), bf16[24,1024,256]{2,1,0:T(8,128)(2,1)}) %all-gather.15.cloned.1.call-update) | async-done | bytes 12582928 | tf_op jit(solution)/shard_map/all_gather | solution.py:14
  1051.7 8.0 reduce_sum.194
  (328 shorter events, 208.1 us)
Async XLA Ops:
  7.2 254.5 %copy-start = (bf16[1024,1024]{1,0:T(8,128)(2,1)S(1)}, bf16[1024,1024]{1,0:T(8,128)(2,1)}, u32[]{:S(2)}) copy-start(bf16[1024,1024]{1,0:T(8,128)(2,1)} %param.27) | copy-start | bytes 6291460
  7.2 58.1 %all-gather.7.cloned.1.call-start = ((), (), s32[]{:S(2)}) async-start(), calls=%async_computation.4 | async-start | bytes 5242880 | tf_op jit(solution)/shard_map/all_gather | solution.py:130
  7.9 196.3 %reduce-scatter.5.cloned.1.call-start = ((), (), s32[]{:S(2)}) async-start(), calls=%async_computation.5 | async-start | bytes 10485760 | tf_op jit(solution)/shard_map/reduce_scatter | solution.py:147
  117.6 86.6 %copy-start.14 = (bf16[512,1024]{1,0:T(8,128)(2,1)S(1)}, bf16[512,1024]{1,0:T(8,128)(2,1)}, u32[]{:S(2)}) copy-start(bf16[512,1024]{1,0:T(8,128)(2,1)} %param.19) | copy-start | bytes 3145732
  117.6 144.1 %all-gather.9.cloned.1.call-start = ((), (), s32[]{:S(2)}) async-start(), calls=%async_computation.6 | async-start | bytes 5242880 | tf_op jit(solution)/shard_map/all_gather | solution.py:157
  118.3 89.2 %copy-start.18 = (f32[1024]{0:T(1024)S(1)}, f32[1024]{0:T(1024)}, u32[]{:S(2)}) copy-start(f32[1024]{0:T(1024)} %param.25) | copy-start | bytes 12292
  118.3 89.2 %copy-start.22 = (f32[1024]{0:T(1024)S(1)}, f32[1024]{0:T(1024)}, u32[]{:S(2)}) copy-start(f32[1024]{0:T(1024)} %param.26) | copy-start | bytes 12292
  208.9 157.0 %reduce-scatter.7.cloned.1.call-start = ((), (), s32[]{:S(2)}) async-start(), calls=%async_computation.7 | async-start | bytes 10485760 | tf_op jit(solution)/shard_map/reduce_scatter | solution.py:158
  261.7 11.0 %copy-start.29 = (bf16[1024,1024]{1,0:T(8,128)(2,1)S(1)}, bf16[1024,1024]{1,0:T(8,128)(2,1)}, u32[]{:S(2)}) copy-start(bf16[1024,1024]{1,0:T(8,128)(2,1)} %param.29) | copy-start | bytes 6291460
  279.3 146.6 %all-gather.11.cloned.1.call-start = ((), (), s32[]{:S(2)}) async-start(), calls=%async_computation.8 | async-start | bytes 5242880 | tf_op jit(solution)/shard_map/all_gather | solution.py:169
  280.0 89.2 %copy-start.9 = (bf16[512,1024]{1,0:T(8,128)(2,1)S(1)}, bf16[512,1024]{1,0:T(8,128)(2,1)}, u32[]{:S(2)}) copy-start(bf16[512,1024]{1,0:T(8,128)(2,1)} %param.33) | copy-start | bytes 3145732
  280.0 89.3 %copy-start.19 = (f32[1024]{0:T(1024)S(1)}, f32[1024]{0:T(1024)}, u32[]{:S(2)}) copy-start(f32[1024]{0:T(1024)} %param.31) | copy-start | bytes 12292
  373.1 159.7 %reduce-scatter.9.cloned.1.call-start = ((), (), s32[]{:S(2)}) async-start(), calls=%async_computation.9 | async-start | bytes 10485760 | tf_op jit(solution)/shard_map/reduce_scatter | solution.py:173
  446.2 86.6 %copy-start.4 = (f32[512,1024]{1,0:T(8,128)S(1)}, f32[512,1024]{1,0:T(8,128)}, u32[]{:S(2)}) copy-start(f32[512,1024]{1,0:T(8,128)} %copy-done.3) | copy-start | bytes 6291460
  446.2 86.6 %copy-start.24 = (f32[1024]{0:T(1024)S(1)}, f32[1024]{0:T(1024)}, u32[]{:S(2)}) copy-start(f32[1024]{0:T(1024)} %param.32) | copy-start | bytes 12292
  446.3 146.3 %all-gather.13.cloned.1.call-start = ((), (), s32[]{:S(2)}) async-start(), calls=%async_computation.10 | async-start | bytes 5242880 | tf_op jit(solution)/shard_map/all_gather | solution.py:184
  539.7 337.7 %all-reduce.5.cloned.1.call-start = ((), (), s32[]{:S(2)}) async-start(), calls=%async_computation.13 | async-start | bytes 9437184 | tf_op jit(solution)/shard_map/psum | solution.py:267
  539.8 9.6 copy-start.28
  539.8 9.6 copy-start.36
  555.4 40.3 %copy-start.17 = (bf16[2,256]{1,0:T(2,128)(2,1)S(1)}, bf16[2,256]{1,0:T(2,128)(2,1)}, u32[]{:S(2)}) copy-start(bf16[2,256]{1,0:T(2,128)(2,1)} %get-tuple-element.547) | copy-start | bytes 3076
  600.3 5.1 copy-start.32
  614.7 7.1 copy-start.31
  642.0 5.1 copy-start.32
  656.4 7.1 copy-start.31
  685.6 5.1 copy-start.32
  700.0 7.1 copy-start.31
  729.2 5.1 copy-start.32
  743.5 7.1 copy-start.31
  769.0 164.5 %reduce-scatter.11.cloned.1.call-start = ((), (), s32[]{:S(2)}) async-start(), calls=%async_computation.11 | async-start | bytes 5242880 | tf_op jit(solution)/shard_map/reduce_scatter | solution.py:261
  776.7 275.0 %all-gather.15.cloned.1.call-start = ((), (), s32[]{:S(2)}) async-start(), calls=%async_computation.12 | async-start | bytes 14155776 | tf_op jit(solution)/shard_map/all_gather | solution.py:14
  883.8 49.7 %copy-start.10 = (f32[512,1024]{1,0:T(8,128)S(1)}, f32[512,1024]{1,0:T(8,128)}, u32[]{:S(2)}) copy-start(f32[512,1024]{1,0:T(8,128)} %get-tuple-element.247) | copy-start | bytes 6291460
  1051.7 11.4 %copy-start.1 = (bf16[1024,1024]{1,0:T(8,128)(2,1)S(1)}, bf16[1024,1024]{1,0:T(8,128)(2,1)}, u32[]{:S(2)}) copy-start(bf16[1024,1024]{1,0:T(8,128)(2,1)} %param.27) | copy-start | bytes 6291460
  (39 other events, 101.8 us)
Sparse Core Ops, SparseCore 0:
  9.9 55.3 all-gather.6
  117.7 86.4 reduce-scatter.4
  209.0 52.6 all-gather.8
  279.4 86.4 reduce-scatter.6
  373.2 52.6 all-gather.10
  446.4 86.4 reduce-scatter.8
  539.8 52.6 all-gather.12
  769.1 108.2 all-reduce.4
  880.7 52.7 reduce-scatter.10
  935.0 116.7 all-gather.14
